TPU v7x, 32 devices: a whole 2x2x4 slice. The times are simulated.
32 devices in a mesh: parts: 2 (over y), row: 4 (over x, core), col: 4 (over z).
Axes of the slice: x: 2, y: 2, z: 4, core: 2. Of those that a mesh axis runs over, the one named last changes fastest.
Arguments:
- left_factor: bfloat16 [6144, 8, 1024], P(('parts', 'col'), None, 'row'), parts along dimension 0, may hold values from -0.109375 to 0.109375
- right_factor: bfloat16 [64, 1024, 3072], P('parts', 'col', 'row'), parts along dimension 0, may hold values from -6 to 6
- amplitudes: bfloat16 [1024, 1024, 512], P('row', 'col', 'parts'), parts along dimension 2, may hold values from -0.0078125 to 0.0078125
Outputs:
- ladder: float32 [512, 256], P(('parts', 'row', 'col')), parts along dimension 0
There are 2 independent parts, one for each index of `parts`. A program takes and returns all parts, laid end to end along the dimension named above; each array names one. Nothing has to cross between parts.
All inputs are finite; a program needn't handle non-finite values.
Results may differ from a plain program's by a relative error of at most 0.0029.
Values may be sent and summed in bfloat16 or wider, within the bound.
A program may use at most 192 MiB of HBM per device.

v0:
```python
import jax
import jax.numpy as jnp
from jax import lax
from jax.sharding import PartitionSpec as P


def contract_aux(left_rows, right_rows):
    return lax.dot_general(
        left_rows, right_rows, (((0,), (1,)), ((), ())), preferred_element_type=jnp.float32
    )


def on_device(left_factor, right_factor, amplitudes):
    width_a = left_factor.shape[1]
    span_c = left_factor.shape[2]
    width_b = right_factor.shape[0]
    span_d = right_factor.shape[1]
    pair_count = amplitudes.shape[2]
    left_all = lax.all_gather(left_factor, "col", axis=0, tiled=True)
    left_flat = left_all.reshape(left_all.shape[0], width_a * span_c)
    shard_part = lax.all_gather(right_factor, "row", axis=2, tiled=True)
    length = shard_part.shape[2]
    integral = contract_aux(left_flat, shard_part.reshape(width_b * span_d, length))
    rounded = integral.astype(jnp.bfloat16).reshape(width_a, span_c, width_b, span_d)
    partial_sums = jnp.einsum(
        "cdp,acbd->pab", amplitudes, rounded, preferred_element_type=jnp.float32
    ).reshape(pair_count, width_a * width_b)
    return lax.psum_scatter(partial_sums, ("row", "col"), scatter_dimension=0, tiled=True)


def solution(mesh):
    return jax.shard_map(
        on_device,
        mesh=mesh,
        in_specs=(
            P(("parts", "col"), None, "row"),
            P("parts", "col", "row"),
            P("row", "col", "parts"),
        ),
        out_specs=P(("parts", "row", "col"), None),
        check_vma=False,
    )
```

profile of v0, /device:TPU:0, one launch (start us, length us, event | category | flops | bytes accessed | tf_op | source)
XLA Modules:
  0.0 753.3 jit_solution(4722424935364290025)
XLA Ops:
  6.5 0.0 all-gather.3.cloned.1.call-start
  6.5 0.7 all-gather.3.cloned.1.call-update
  7.3 0.0 all-gather.5.cloned.1.call-start
  7.3 0.7 all-gather.5.cloned.1.call-update
  8.0 0.0 reduce-scatter.2.cloned.1.call-start
  8.1 221.8 %all-gather.3.cloned.1.call-done = bf16[3072,8,256]{2,1,0:T(8,128)(2,1)} async-done(((bf16[768,8,256]{2,1,0:T(8,128)(2,1)}), bf16[3072,8,256]{2,1,0:T(8,128)(2,1)}) %all-gather.3.cloned.1.call-update) | async-done | bytes 12582928 | tf_op jit(solution)/shard_map/all_gather | solution.py:19
  229.8 13.5 %copy.7 = bf16[384,8,8,256]{3,1,2,0:T(8,128)(2,1)} copy(bf16[384,8,8,256]{3,2,1,0:T(8,128)(2,1)} %bitcast.23) | data formatting | bytes 25165824
  243.3 285.9 %all-gather.5.cloned.1.call-done = bf16[32,256,3072]{2,1,0:T(8,128)(2,1)} async-done(((bf16[32,256,768]{2,1,0:T(8,128)(2,1)}), bf16[32,256,3072]{2,1,0:T(8,128)(2,1)}) %all-gather.5.cloned.1.call-update) | async-done | bytes 50331664 | tf_op jit(solution)/shard_map/all_gather | solution.py:21
  529.2 115.1 %convolution_convert_fusion = bf16[2048,8192]{1,0:T(8,128)(2,1)} fusion(bf16[3072,2048]{1,0:T(8,128)(2,1)} %bitcast.24, bf16[8192,3072]{1,0:T(8,128)(2,1)} %bitcast.26), kind=kOutput, calls=%fused_computation.3 | convolution fusion | flops 103095992320 | bytes 96468992 | tf_op jit(solution)/shard_map/dot_general | solution.py:8
  644.3 23.0 %copy.8 = bf16[256,8,32,256]{3,2,1,0:T(8,128)(2,1)} copy(bf16[256,8,32,256]{3,1,2,0:T(8,128)(2,1)} %bitcast.22) | data formatting | bytes 67108864
  667.3 22.7 %fusion = f32[8,32,256,1]{2,1,3,0:T(8,128)S(1)} fusion(bf16[256,256,256]{2,1,0:T(8,128)(2,1)} %param.5, bf16[8,256,32,256]{3,2,1,0:T(8,128)(2,1)} %bitcast.21), kind=kOutput, calls=%fused_computation | convolution fusion | flops 8589934592 | bytes 67371008 | tf_op jit(solution)/shard_map/cdp,acbd->pab/dot_general | solution.py:25
  690.0 0.8 copy.5
  690.9 0.0 reduce-scatter.2.cloned.1.call-update
  690.9 55.9 %reduce-scatter.2.cloned.1.call-done = f32[16,256]{1,0:T(8,128)} async-done(((f32[256,256]{1,0:T(8,128)}), f32[16,256]{1,0:T(8,128)}) %reduce-scatter.2.cloned.1.call-update) | async-done | bytes 16400 | tf_op jit(solution)/shard_map/reduce_scatter | solution.py:28
Async XLA Ops:
  6.5 223.3 %all-gather.3.cloned.1.call-start = ((), (), s32[]{:S(2)}) async-start(), calls=%async_computation.1 | async-start | bytes 15728640 | tf_op jit(solution)/shard_map/all_gather | solution.py:19
  7.3 521.9 %all-gather.5.cloned.1.call-start = ((), (), s32[]{:S(2)}) async-start(), calls=%async_computation.2 | async-start | bytes 62914560 | tf_op jit(solution)/shard_map/all_gather | solution.py:21
  8.0 738.8 %reduce-scatter.2.cloned.1.call-start = ((), (), s32[]{:S(2)}) async-start(), calls=%async_computation.3 | async-start | bytes 278528 | tf_op jit(solution)/shard_map/reduce_scatter | solution.py:28
Sparse Core Ops, SparseCore 0:
  8.9 220.8 all-gather.2
  231.4 297.7 all-gather.4
  691.0 55.7 reduce-scatter.1
where the time goes:
time: 754 us; the launch traced here: 753 us
  waiting for transfers between devices  565 us (75%)
  matrix products  138 us (18%)
  local copies, waits for them, and re-layouts  37.4 us (5%)
  between operations  13.1 us (2%)
    all_gather x1, waiting for transfers between devices, on_device(): shard_part = lax.all_gather(right_factor, 'row', axis=2, tiled=True)  286 us
    all_gather x1, waiting for transfers between devices, on_device(): left_all = lax.all_gather(left_factor, 'col', axis=0, tiled=True)  222 us
    dot_general x1, matrix products, contract_aux(): lax.dot_general(left_rows, right_rows, (((0,), (1,)), ((), ())), preferre...  115 us
    reduce_scatter x1, waiting for transfers between devices, on_device(): lax.psum_scatter(partial_sums, ('row', 'col'), scatter_dimension=0, tiled...  55.9 us
    unnamed x2, local copies, waits for them, and re-layouts  36.5 us
    dot_general x1, matrix products, on_device(): jnp.einsum('cdp,acbd->pab', amplitudes, rounded, preferred_element_type=j...  22.7 us
  transfers between devices with their start and end apart: 3, of which 3 were waited for; matrix products, arithmetic and copies ran while one was open for 2% of the time, Pallas kernels for 0%

commit v1 on v0

--- a/solution.py
+++ b/solution.py
@@ -16,7 +16,14 @@
     width_b = right_factor.shape[0]
     span_d = right_factor.shape[1]
     pair_count = amplitudes.shape[2]
-    left_all = lax.all_gather(left_factor, "col", axis=0, tiled=True)
+    ways, here, step = (lax.axis_size("col"), lax.axis_index("col"), left_factor.shape[0])
+    line, have = (left_factor, 1)
+    while have < ways:
+        line = jnp.concatenate(
+            [line, lax.ppermute(line, "col", [(d, (d - have) % ways) for d in range(ways)])], axis=0
+        )
+        have = 2 * have
+    left_all = jnp.roll(line, here * step, axis=0)
     left_flat = left_all.reshape(left_all.shape[0], width_a * span_c)
     shard_part = lax.all_gather(right_factor, "row", axis=2, tiled=True)
     length = shard_part.shape[2]

time: 754 us -> 605 us (0.80)
  waiting for transfers between devices: 565 us -> 393 us
  other arithmetic: 0 us -> 9.02 us
    ppermute x0 -> x2, waiting for transfers between devices: none -> 336 us  [on_device(): lax.ppermute(line, 'col', [(d, (d - have) % ways) for d in range(ways)])]
    all_gather x1, waiting for transfers between devices: 286 us -> 0.01 us  [on_device(): shard_part = lax.all_gather(right_factor, 'row', axis=2, tiled=True)]
    all_gather x1 -> x0, waiting for transfers between devices: 222 us -> none  [on_device(): left_all = lax.all_gather(left_factor, 'col', axis=0, tiled=True)]
    concatenate x0 -> x1, other arithmetic: none -> 9.02 us  [on_device(): jnp.concatenate([line, lax.ppermute(line, 'col', [(d, (d - have) % ways)...]
    unnamed x2 -> x13, local copies, waits for them, and re-layouts: 36.5 us -> 39 us
  transfers between devices with their start and end apart: 3 -> 4, of which waited for: 3 -> 3; matrix products, arithmetic and copies ran while one was open for 2% -> 5% of each run, Pallas kernels for 0% -> 0%
where the time goes in v1:
time: 605 us; the launch traced here: 604 us
  waiting for transfers between devices  393 us (65%)
  matrix products  138 us (23%)
  local copies, waits for them, and re-layouts  44.6 us (7%)
  between operations  13.5 us (2%)
  other arithmetic  9.02 us (1%)
  starting transfers between devices  6.53 us (1%)
    ppermute x2, waiting for transfers between devices, on_device(): lax.ppermute(line, 'col', [(d, (d - have) % ways) for d in range(ways)])  336 us
    dot_general x1, matrix products, contract_aux(): lax.dot_general(left_rows, right_rows, (((0,), (1,)), ((), ())), preferre...  115 us
    reduce_scatter x1, waiting for transfers between devices, on_device(): lax.psum_scatter(partial_sums, ('row', 'col'), scatter_dimension=0, tiled...  55.9 us
    unnamed x13, local copies, waits for them, and re-layouts  39 us
    dot_general x1, matrix products, on_device(): jnp.einsum('cdp,acbd->pab', amplitudes, rounded, preferred_element_type=j...  22.7 us
  transfers between devices with their start and end apart: 4, of which 3 were waited for; matrix products, arithmetic and copies ran while one was open for 5% of the time, Pallas kernels for 0%

profile of v1, /device:TPU:0, one launch (start us, length us, event | category | flops | bytes accessed | tf_op | source)
XLA Modules:
  0.0 604.4 jit_solution(13533256620622418636)
XLA Ops:
  6.5 0.0 copy-start
  6.5 0.0 all-gather.2.cloned.1.call-start
  6.5 0.7 all-gather.2.cloned.1.call-update
  7.3 0.0 reduce-scatter.2.cloned.1.call-start
  7.3 5.1 collective-permute-start
  12.4 67.7 %collective-permute-done = bf16[768,8,256]{2,1,0:T(8,128)(2,1)S(1)} collective-permute-done((bf16[768,8,256]{2,1,0:T(8,128)(2,1)}, bf16[768,8,256]{2,1,0:T(8,128)(2,1)S(1)}, u32[]{:S(2)}, u32[]{:S(2)}) %collective-permute-start) | collective-permute-done | bytes 3145760 | tf_op jit(solution)/shard_map/ppermute | solution.py:23
  80.1 0.0 copy-start.1
  80.1 1.6 copy-done.1
  81.7 9.0 %pad_maximum_fusion = bf16[1536,8,256]{2,1,0:T(8,128)(2,1)} fusion(bf16[768,8,256]{2,1,0:T(8,128)(2,1)S(1)} %collective-permute-done, bf16[768,8,256]{2,1,0:T(8,128)(2,1)} %param.3), kind=kLoop, calls=%fused_computation.4 | loop fusion | flops 3145728 | bytes 12582912 | tf_op jit(solution)/shard_map/concatenate | solution.py:22
  90.8 1.4 collective-permute-start.1
  92.1 0.0 copy-done
  92.1 0.0 copy-start.2
  92.1 0.2 constant_dynamic-update-slice_fusion.5
  92.3 2.2 constant_dynamic-update-slice_fusion.4
  94.6 268.6 %collective-permute-done.1 = bf16[1536,8,256]{2,1,0:T(8,128)(2,1)} collective-permute-done((bf16[1536,8,256]{2,1,0:T(8,128)(2,1)}, bf16[1536,8,256]{2,1,0:T(8,128)(2,1)}, u32[]{:S(2)}, u32[]{:S(2)}) %collective-permute-start.1) | collective-permute-done | bytes 6291488 | tf_op jit(solution)/shard_map/ppermute | solution.py:23
  363.2 3.8 constant_dynamic-update-slice_fusion.3
  367.0 0.2 constant_dynamic-update-slice_fusion.2
  367.3 0.0 copy-done.2
  367.3 0.2 constant_dynamic-update-slice_fusion.1
  367.5 3.8 constant_dynamic-update-slice_fusion
  371.3 0.9 constant_dynamic-slice_fusion
  372.2 7.6 %copy.6 = bf16[384,8,8,256]{3,1,2,0:T(8,128)(2,1)} copy(bf16[384,8,8,256]{3,2,1,0:T(8,128)(2,1)S(1)} %bitcast.22) | data formatting | bytes 25165824
  379.8 0.0 all-gather.2.cloned.1.call-done
  379.8 115.2 %convolution_convert_fusion = bf16[2048,8192]{1,0:T(8,128)(2,1)} fusion(bf16[3072,2048]{1,0:T(8,128)(2,1)} %bitcast.24, bf16[8192,3072]{1,0:T(8,128)(2,1)} %bitcast.26), kind=kOutput, calls=%fused_computation.3 | convolution fusion | flops 103095992320 | bytes 96468992 | tf_op jit(solution)/shard_map/dot_general | solution.py:8
  495.0 23.1 %copy.7 = bf16[256,8,32,256]{3,2,1,0:T(8,128)(2,1)} copy(bf16[256,8,32,256]{3,1,2,0:T(8,128)(2,1)} %bitcast.23) | data formatting | bytes 67108864
  518.1 22.7 %fusion = f32[8,32,256,1]{2,1,3,0:T(8,128)S(1)} fusion(bf16[256,256,256]{2,1,0:T(8,128)(2,1)} %param.5, bf16[8,256,32,256]{3,2,1,0:T(8,128)(2,1)} %bitcast.21), kind=kOutput, calls=%fused_computation | convolution fusion | flops 8589934592 | bytes 67371008 | tf_op jit(solution)/shard_map/cdp,acbd->pab/dot_general | solution.py:32
  540.8 0.8 copy.4
  541.6 0.0 reduce-scatter.2.cloned.1.call-update
  541.6 55.9 %reduce-scatter.2.cloned.1.call-done = f32[16,256]{1,0:T(8,128)} async-done(((f32[256,256]{1,0:T(8,128)}), f32[16,256]{1,0:T(8,128)}) %reduce-scatter.2.cloned.1.call-update) | async-done | bytes 16400 | tf_op jit(solution)/shard_map/reduce_scatter | solution.py:35
Async XLA Ops:
  6.5 85.6 %copy-start = (bf16[768,8,256]{2,1,0:T(8,128)(2,1)S(1)}, bf16[768,8,256]{2,1,0:T(8,128)(2,1)}, u32[]{:S(2)}) copy-start(bf16[768,8,256]{2,1,0:T(8,128)(2,1)} %param.3) | copy-start | bytes 9437188
  6.5 373.3 %all-gather.2.cloned.1.call-start = ((), (), s32[]{:S(2)}) async-start(), calls=%async_computation.1 | async-start | bytes 62914560 | tf_op jit(solution)/shard_map/all_gather | solution.py:28
  7.3 590.3 %reduce-scatter.2.cloned.1.call-start = ((), (), s32[]{:S(2)}) async-start(), calls=%async_computation.2 | async-start | bytes 278528 | tf_op jit(solution)/shard_map/reduce_scatter | solution.py:35
  7.3 72.8 %collective-permute-start = (bf16[768,8,256]{2,1,0:T(8,128)(2,1)}, bf16[768,8,256]{2,1,0:T(8,128)(2,1)S(1)}, u32[]{:S(2)}, u32[]{:S(2)}) collective-permute-start(bf16[768,8,256]{2,1,0:T(8,128)(2,1)} %param.3), channel_id=1, source_target_pairs={{0,3},{1,0},{2,1},{3,2},{4,7},{5,4},{6,5},{7,6},{8,11},{9,8},{10,9... | collective-permute-start | bytes 9437192 | tf_op jit(solution)/shard_map/ppermute | solution.py:23
  80.1 1.6 copy-start.1
  90.8 272.4 %collective-permute-start.1 = (bf16[1536,8,256]{2,1,0:T(8,128)(2,1)}, bf16[1536,8,256]{2,1,0:T(8,128)(2,1)}, u32[]{:S(2)}, u32[]{:S(2)}) collective-permute-start(bf16[1536,8,256]{2,1,0:T(8,128)(2,1)} %pad_maximum_fusion), channel_id=1, source_target_pairs={{0,2},{1,3},{2,0},{3,1},{4,6},{5,7},{6,4},{7,5},{8,10},{9,11},{10,... | collective-permute-start | bytes 18874376 | tf_op jit(solution)/shard_map/ppermute | solution.py:23
  92.1 275.1 %copy-start.2 = (bf16[768,8,256]{2,1,0:T(8,128)(2,1)S(1)}, bf16[768,8,256]{2,1,0:T(8,128)(2,1)}, u32[]{:S(2)}) copy-start(bf16[768,8,256]{2,1,0:T(8,128)(2,1)} %copy-done.1) | copy-start | bytes 9437188
Sparse Core Ops, SparseCore 0:
  8.9 302.2 all-gather.1
  541.7 55.7 reduce-scatter.1
